TPU v7x, 32 devices: a whole 2x2x4 slice. The times are simulated.
32 devices in a mesh: bulk: 4 (over z), expert: 8 (over y, x, core).
Axes of the slice: x: 2, y: 2, z: 4, core: 2. Of those that a mesh axis runs over, the one named last changes fastest.
Arguments:
- tokens: bfloat16 [2048, 7168], P(('bulk', 'expert')), may hold values from -6 to 6
- expert_ids: int32 [2048, 8], P(('bulk', 'expert')), may hold values from 0 to 255, all different within a row; in each aligned block of 64 rows (0 to 63, 64 to 127, ...) at most 3 rows name the same one
- gate_values: float32 [2048, 8], P(('bulk', 'expert')), may hold values from 0.25 to 2.5
- placement: int32 [8], replicated, may hold values from 0 to 7, as said below
- gate_weight: bfloat16 [8, 7168, 2048], P('expert', 'bulk'), may hold values from -0.0625 to 0.0625
- up_weight: bfloat16 [8, 7168, 2048], P('expert', 'bulk'), may hold values from -0.0625 to 0.0625
- down_weight: bfloat16 [8, 2048, 7168], P('expert', None, 'bulk'), may hold values from -0.125 to 0.125
Outputs:
- layer_out: bfloat16 [2048, 7168], P(('bulk', 'expert'))
- host_load: int32 [32, 8], P(('bulk', 'expert'))
Inputs may be any that keep to these rules, and one draw needn't show every extreme that they name: `expert_ids`: in each aligned block of 64 rows (the tokens of one device) no expert is named by more than 3 rows; a token names an expert at most once. Exactly one expert e has placement[e] != e: its home device e is power-capped and its host is the next device of the expert axis, placement[e] = (e + 1) mod 8; every other expert stays on its home device.
All inputs are finite; a program needn't handle non-finite values.
Results may differ from a plain program's by a relative error of at most 0.018.
Values may be sent and summed in bfloat16 or wider, within the bound.
A program may use at most 128 MiB of HBM per device.

v0:
```python
import jax
import jax.numpy as jnp
from jax import lax
from jax.sharding import PartitionSpec as P

CAP = 3


def passed_along(value, axis, by):
    devices = lax.axis_size(axis)
    return lax.ppermute(value, axis, [(i, (i + by) % devices) for i in range(devices)])


def gather_rows(tokens, slot_of_pair, slot_count, tok_rows, top_count):
    selector = (jnp.arange(slot_count, dtype=jnp.int32)[:, None] == slot_of_pair[None, :]).astype(
        jnp.bfloat16
    )
    selector = jnp.sum(selector.reshape(slot_count, tok_rows, top_count), axis=2)
    return jnp.dot(selector, tokens, preferred_element_type=jnp.float32).astype(jnp.bfloat16)


def expert_rows(grouped, weight_blocks, hidden_width):
    bulk_count, per_group, slice_width = grouped.shape
    pieces = []
    offset = 0
    for partial_block_rows, partial_weights_now in weight_blocks:
        block_input = grouped[:, offset : offset + partial_block_rows]
        offset += partial_block_rows
        gate_part = jnp.einsum(
            "grd,df->grf", block_input, partial_weights_now[0], preferred_element_type=jnp.float32
        )
        up_part = jnp.einsum(
            "grd,df->grf", block_input, partial_weights_now[1], preferred_element_type=jnp.float32
        )
        pieces.append(jnp.concatenate([gate_part, up_part], axis=2))
    summed = lax.psum_scatter(
        jnp.concatenate(pieces, axis=1)
        .reshape(per_group * lax.axis_size("bulk"), 2 * hidden_width)
        .astype(jnp.bfloat16),
        "bulk",
        scatter_dimension=0,
        tiled=True,
    ).astype(jnp.float32)
    hidden = (jax.nn.silu(summed[:, :hidden_width]) * summed[:, hidden_width:]).astype(jnp.bfloat16)
    all_hidden = lax.all_gather(hidden, "bulk", axis=0, tiled=True).reshape(
        bulk_count, per_group, hidden_width
    )
    outputs = []
    offset = 0
    for block_rows, weights_now in weight_blocks:
        block_hidden = all_hidden[:, offset : offset + block_rows]
        offset += block_rows
        outputs.append(
            jnp.einsum(
                "grf,fd->grd", block_hidden, weights_now[2], preferred_element_type=jnp.float32
            ).astype(jnp.bfloat16)
        )
    return jnp.concatenate(outputs, axis=1)


def on_device(tokens, expert_ids, gate_values, placement, gate_weight, up_weight, down_weight):
    expert_count = lax.axis_size("expert")
    bulk_count = lax.axis_size("bulk")
    tok_rows, top_count = expert_ids.shape
    model_width = tokens.shape[1]
    slice_width = model_width // bulk_count
    hidden_width = gate_weight.shape[2]
    pair_count = tok_rows * top_count
    slot_count = expert_count * CAP
    expert_iota = jnp.arange(expert_count, dtype=jnp.int32)
    is_moved = placement != expert_iota
    flat_ids = expert_ids.reshape(pair_count)
    flat_gates = gate_values.reshape(pair_count)
    is_live = flat_ids < expert_count
    safe_ids = jnp.where(is_live, flat_ids, 0)
    membership = ((safe_ids[:, None] == expert_iota[None, :]) & is_live[:, None]).astype(jnp.int32)
    rank_table = jnp.cumsum(membership, axis=0) - 1
    position = jnp.sum(rank_table * membership, axis=1)
    row_within = jnp.arange(pair_count, dtype=jnp.int32) // top_count
    moved_pair = jnp.sum(membership * is_moved.astype(jnp.int32)[None, :], axis=1) > 0
    replica_dev = (safe_ids + 1) % expert_count
    to_replica = is_live & (moved_pair | (row_within % 2 == 1))
    destination = jnp.where(to_replica, replica_dev, safe_ids)
    load_table = jnp.sum(
        ((destination[:, None] == expert_iota[None, :]) & is_live[:, None]).astype(jnp.int32),
        axis=0,
    )[None, :]
    own_weights = (gate_weight[0], up_weight[0], down_weight[0])
    spread_slot = jnp.where(is_live, safe_ids * CAP + position, -1)
    kind_count = 1
    outgoing = gather_rows(tokens, spread_slot, kind_count * slot_count, tok_rows, top_count)
    outgoing = outgoing.reshape(kind_count, expert_count, CAP, model_width)
    arrived = lax.all_to_all(
        lax.all_to_all(outgoing, "bulk", split_axis=3, concat_axis=0, tiled=True),
        "expert",
        split_axis=1,
        concat_axis=1,
        tiled=True,
    )
    grouped = arrived.reshape(bulk_count, kind_count * slot_count, slice_width)
    weight_blocks = ((slot_count, own_weights),)
    results = expert_rows(grouped, weight_blocks, hidden_width)
    main_part = results.reshape(bulk_count * kind_count, expert_count, CAP, slice_width)
    returned = lax.all_to_all(
        lax.all_to_all(main_part, "bulk", split_axis=0, concat_axis=3, tiled=True),
        "expert",
        split_axis=1,
        concat_axis=1,
        tiled=True,
    )
    returned = returned.reshape(kind_count * slot_count, model_width)
    picked = jnp.take(returned, jnp.maximum(spread_slot, 0), axis=0)
    pair_scale = jnp.where(is_live, flat_gates, 0.0)
    weighted = picked.astype(jnp.float32) * pair_scale[:, None]
    layer_out = jnp.sum(weighted.reshape(tok_rows, top_count, model_width), axis=1).astype(
        jnp.bfloat16
    )
    return (layer_out, load_table)


def solution(mesh):
    placed = (
        P(("bulk", "expert"), None),
        P(("bulk", "expert"), None),
        P(("bulk", "expert"), None),
        P(),
        P("expert", "bulk", None),
        P("expert", "bulk", None),
        P("expert", None, "bulk"),
    )
    return jax.shard_map(
        on_device,
        mesh=mesh,
        in_specs=placed,
        out_specs=(P(("bulk", "expert"), None), P(("bulk", "expert"), None)),
        check_vma=False,
    )
```

profile of v0, /device:TPU:0, one launch (start us, length us, event | category | flops | bytes accessed | tf_op | source)
XLA Modules:
  0.0 176.0 jit_solution(6337480197885202677)
XLA Ops:
  7.2 0.0 copy-start
  7.2 0.0 reduce-scatter.2.cloned.1.call-start
  7.2 0.8 copy.56
  8.1 0.1 reshape.195
  8.2 0.1 reshape.194
  8.3 0.7 compare_convert_fusion
  8.9 1.1 reduce-window.6
  10.1 0.2 slice_reduce_fusion
  10.3 0.1 select_reduce_fusion
  10.5 0.1 reduce_sum.53
  10.6 0.1 copy.60
  10.6 0.1 fusion.19
  10.7 0.0 copy-done
  10.7 0.2 convolution_convert_fusion
  10.9 0.2 reshape.197
  11.2 7.3 %copy.61 = bf16[1,8,3,7168]{1,2,0,3:T(4,128)(2,1)} copy(bf16[1,8,3,7168]{3,2,1,0:T(4,128)(2,1)S(1)} %reshape.197) | data formatting | bytes 688128 | tf_op jit(solution)/shard_map/reshape | solution.py:92
  18.4 7.8 %reshape.216 = bf16[4,2,21504]{2,1,0:T(2,128)(2,1)S(1)} reshape(bf16[7168,1,3,8]{3,2,1,0:T(4,128)(2,1)} %bitcast.50) | data formatting | bytes 688128
  26.3 16.7 %all_to_all.46 = bf16[4,2,21504]{2,1,0:T(2,128)(2,1)S(1)} all-to-all(bf16[4,2,21504]{2,1,0:T(2,128)(2,1)S(1)} %reshape.216), channel_id=1, replica_groups=mesh['bulk'=4,'expert'=8] {'bulk'}, dimensions={0} | all-to-all | bytes 688128 | tf_op jit(solution)/shard_map/all_to_all | solution.py:94
  43.0 8.2 %reshape.217 = bf16[7168,1,3,8]{3,2,1,0:T(4,128)(2,1)} reshape(bf16[4,2,21504]{2,1,0:T(2,128)(2,1)S(1)} %all_to_all.46) | data formatting | bytes 688128
  51.2 9.9 %copy.63 = bf16[4,8,3,1792]{3,0,2,1:T(4,128)(2,1)S(1)} copy(bf16[4,8,3,1792]{1,2,3,0:T(4,128)(2,1)} %bitcast.51) | data formatting | bytes 688128 | tf_op jit(solution)/shard_map/all_to_all | solution.py:94
  61.2 11.3 %all_to_all.47 = bf16[4,8,3,1792]{3,0,2,1:T(4,128)(2,1)S(1)} all-to-all(bf16[4,8,3,1792]{3,0,2,1:T(4,128)(2,1)S(1)} %copy.63), channel_id=1, replica_groups=mesh['bulk'=4,'expert'=8] {'expert'}, dimensions={1} | all-to-all | bytes 688128 | tf_op jit(solution)/shard_map/all_to_all | solution.py:93
  72.5 0.0 copy-start.1
  72.5 4.4 %fusion.9 = bf16[4,24,2048]{2,1,0:T(8,128)(2,1)S(1)} fusion(bf16[1,1792,2048]{2,1,0:T(8,128)(2,1)} %param.12, bf16[4,24,1792]{2,0,1:T(4,128)(2,1)S(1)} %bitcast.53), kind=kOutput, calls=%fused_computation.11 | convolution fusion | flops 704839680 | bytes 8077312 | tf_op jit(solution)/shard_map/grd,df->grf/dot_general | solution.py:32
  76.9 4.4 %fusion.6 = bf16[4,24,2048]{2,1,0:T(8,128)(2,1)S(1)} fusion(bf16[1,1792,2048]{2,1,0:T(8,128)(2,1)} %param.11, bf16[4,24,1792]{2,0,1:T(4,128)(2,1)S(1)} %bitcast.54), kind=kOutput, calls=%fused_computation.10 | convolution fusion | flops 704839680 | bytes 8077312 | tf_op jit(solution)/shard_map/grd,df->grf/dot_general | solution.py:29
  81.4 0.9 pad_maximum_fusion
  82.3 0.0 reduce-scatter.2.cloned.1.call-update
  82.3 0.1 reshape.202
  82.4 0.0 copy-done.1
  82.4 0.1 copy.71
  82.5 20.5 %reduce-scatter.2.cloned.1.call-done = bf16[24,4096]{1,0:T(8,128)(2,1)} async-done(((bf16[96,4096]{1,0:T(8,128)(2,1)}), bf16[24,4096]{1,0:T(8,128)(2,1)}) %reduce-scatter.2.cloned.1.call-update) | async-done | bytes 196624 | tf_op jit(solution)/shard_map/reduce_scatter | solution.py:36
  103.0 1.0 convert_element_type.44
  104.0 0.1 fusion.17
  104.1 15.0 %all_gather.3 = bf16[96,2048]{1,0:T(8,128)(2,1)S(1)} all-gather(bf16[24,2048]{1,0:T(8,128)(2,1)S(1)} %fusion.17), channel_id=1, replica_groups=mesh['bulk'=4,'expert'=8] {'bulk'}, dimensions={0}, use_global_device_ids=true | all-gather | bytes 491520 | tf_op jit(solution)/shard_map/all_gather | solution.py:45
  119.0 4.4 %fusion.12 = bf16[4,24,1792]{2,1,0:T(8,128)(2,1)S(1)} fusion(bf16[4,24,2048]{2,1,0:T(8,128)(2,1)S(1)} %bitcast.55, bf16[1,2048,1792]{2,1,0:T(8,128)(2,1)} %param.13), kind=kOutput, calls=%fused_computation.12 | convolution fusion | flops 704815104 | bytes 8077312 | tf_op jit(solution)/shard_map/grf,fd->grd/dot_general | solution.py:54
  123.4 0.1 copy.66
  123.6 0.8 copy.67
  124.3 3.5 %all-to-all-start.2 = ((bf16[4,8,3,1792]{3,1,2,0:T(8,128)(2,1)}), bf16[4,8,3,1792]{3,1,2,0:T(8,128)(2,1)S(1)}, u32[]{:S(2)}, u32[]{:S(2)}) async-start(bf16[4,8,3,1792]{3,1,2,0:T(8,128)(2,1)} %copy.67), calls=%async_computation.3 | async-start | bytes 688128 | tf_op jit(solution)/shard_map/all_to_all | solution.py:105
  127.8 0.6 convert_reduce_fusion
  128.5 6.8 %all-to-all-done.2 = bf16[4,8,3,1792]{3,1,2,0:T(8,128)(2,1)S(1)} async-done(((bf16[4,8,3,1792]{3,1,2,0:T(8,128)(2,1)}), bf16[4,8,3,1792]{3,1,2,0:T(8,128)(2,1)S(1)}, u32[]{:S(2)}, u32[]{:S(2)}) %all-to-all-start.2) | async-done | bytes 344096 | tf_op jit(solution)/shard_map/all_to_all | solution.py:105
  135.2 0.1 copy.74
  135.3 0.9 reshape.214
  136.3 3.7 %all-to-all-start.3 = ((bf16[1,8,3,7168]{3,2,0,1:T(4,128)(2,1)}), bf16[1,8,3,7168]{3,2,0,1:T(4,128)(2,1)S(1)}, u32[]{:S(2)}, u32[]{:S(2)}) async-start(bf16[1,8,3,7168]{3,2,0,1:T(4,128)(2,1)} %reshape.214), calls=%async_computation.4 | async-start | bytes 917504 | tf_op jit(solution)/shard_map/all_to_all | solution.py:104
  140.0 9.0 %all-to-all-done.3 = bf16[1,8,3,7168]{3,2,0,1:T(4,128)(2,1)S(1)} async-done(((bf16[1,8,3,7168]{3,2,0,1:T(4,128)(2,1)}), bf16[1,8,3,7168]{3,2,0,1:T(4,128)(2,1)S(1)}, u32[]{:S(2)}, u32[]{:S(2)}) %all-to-all-start.3) | async-done | bytes 344096 | tf_op jit(solution)/shard_map/all_to_all | solution.py:104
  149.0 0.3 reshape.201
  149.3 7.1 %gather_fusion = bf16[512,7168]{1,0:T(8,128)(2,1)} fusion(bf16[24,7168]{1,0:T(8,128)(2,1)S(1)} %reshape.201, s32[1024]{0:T(1024)S(1)} %pad_clamp_fusion), kind=kCustom, calls=%fused_computation | custom fusion | bytes 14682112 | tf_op jit(solution)/shard_map/jit(_take)/gather | solution.py:112
  156.4 12.8 %multiply_reduce_fusion = bf16[64,7168]{1,0:T(8,128)(2,1)} fusion(bf16[512,7168]{1,0:T(8,128)(2,1)} %gather_fusion, f32[64,8]{1,0:T(8,128)S(1)} %compare_select_fusion, pred[64,8]{1,0:T(8,128)(4,1)S(1)} %get-tuple-element.4), kind=kLoop, calls=%fused_computation.1 | loop fusion | flops 14221312 | bytes 8260096 | tf_op jit(solution)/shard_map/reduce_sum | solution.py:115
  (11 shorter events, 0.1 us)
Async XLA Ops:
  7.2 3.5 %copy-start = (bf16[64,7168]{1,0:T(8,128)(2,1)S(1)}, bf16[64,7168]{1,0:T(8,128)(2,1)}, u32[]{:S(2)}) copy-start(bf16[64,7168]{1,0:T(8,128)(2,1)} %param.7) | copy-start | bytes 2752516
  7.2 95.8 %reduce-scatter.2.cloned.1.call-start = ((), (), s32[]{:S(2)}) async-start(), calls=%async_computation.5 | async-start | bytes 983040 | tf_op jit(solution)/shard_map/reduce_scatter | solution.py:36
  72.5 9.9 %copy-start.1 = (f32[64,8]{0,1:T(8,128)S(1)}, f32[64,8]{0,1:T(8,128)}, u32[]{:S(2)}) copy-start(f32[64,8]{0,1:T(8,128)} %param.9) | copy-start | bytes 6148
  124.3 10.9 %all-to-all-start.2 = ((bf16[4,8,3,1792]{3,1,2,0:T(8,128)(2,1)}), bf16[4,8,3,1792]{3,1,2,0:T(8,128)(2,1)S(1)}, u32[]{:S(2)}, u32[]{:S(2)}) async-start(bf16[4,8,3,1792]{3,1,2,0:T(8,128)(2,1)} %copy.67), calls=%async_computation.3 | async-start | bytes 688128 | tf_op jit(solution)/shard_map/all_to_all | solution.py:105
  136.3 12.8 %all-to-all-start.3 = ((bf16[1,8,3,7168]{3,2,0,1:T(4,128)(2,1)}), bf16[1,8,3,7168]{3,2,0,1:T(4,128)(2,1)S(1)}, u32[]{:S(2)}, u32[]{:S(2)}) async-start(bf16[1,8,3,7168]{3,2,0,1:T(4,128)(2,1)} %reshape.214), calls=%async_computation.4 | async-start | bytes 917504 | tf_op jit(solution)/shard_map/all_to_all | solution.py:104
Sparse Core Ops, SparseCore 0:
  82.4 20.5 reduce-scatter.1
where the time goes:
time: 177 us; the launch traced here: 176 us
  local copies, waits for them, and re-layouts  44.3 us (25%)
  blocking collectives  43 us (24%)
  waiting for transfers between devices  36.3 us (21%)
  other arithmetic  17.4 us (10%)
  between operations  14.2 us (8%)
  matrix products  13.5 us (8%)
  starting transfers between devices  7.24 us (4%)
    reduce_scatter x1, waiting for transfers between devices, expert_rows(): lax.psum_scatter(jnp.concatenate(pieces, axis=1).reshape(per_group * lax....  20.5 us
    unnamed x8, local copies, waits for them, and re-layouts  17 us
    all_to_all x1, blocking collectives, on_device(): lax.all_to_all(outgoing, 'bulk', split_axis=3, concat_axis=0, tiled=True)  16.7 us
    all_gather x1, blocking collectives, expert_rows(): lax.all_gather(hidden, 'bulk', axis=0, tiled=True)  15 us
    reduce_sum x1, other arithmetic, on_device(): jnp.sum(weighted.reshape(tok_rows, top_count, model_width), axis=1)  12.8 us
    all_to_all x1, blocking collectives, on_device(): lax.all_to_all(lax.all_to_all(outgoing, 'bulk', split_axis=3, concat_axis...  11.3 us
    all_to_all x1, local copies, waits for them, and re-layouts, on_device(): lax.all_to_all(outgoing, 'bulk', split_axis=3, concat_axis=0, tiled=True)  9.94 us
    all_to_all x1, waiting for transfers between devices, on_device(): lax.all_to_all(lax.all_to_all(main_part, 'bulk', split_axis=0, concat_axi...  9.02 us
  transfers between devices with their start and end apart: 3, of which 3 were waited for; matrix products, arithmetic and copies ran while one was open for 0% of the time, Pallas kernels for 0%

commit v1 on v0

v1 whole, which is shorter than its diff:
```python
import functools

import jax
import jax.numpy as jnp
import ml_dtypes
import numpy as np
from jax import lax
from jax.experimental import pallas as pl
from jax.experimental.pallas import tpu as pltpu
from jax.sharding import PartitionSpec as P

CAP = 3
BF = jnp.bfloat16
F32 = jnp.float32
MESH = pl.DeviceIdType.MESH


def dot(a, b):
    return jnp.dot(a, b, preferred_element_type=F32)


def kernel(
    B, E, RP, tok, ids, gv, place, p1, p1t, p2, p2t, wg_hbm, wu_hbm, wd_hbm, out, load,
    wg, wu, wd, og, oin, xs, xr, x, pout, pin, hin, acc, back, rb, fin,
    wsem, s1, r1, s2, r2, s3, r3, s4, r4, s5, r5, s6, r6,
):
    T, TOP = ids.shape
    SL = E * CAP
    DS = wg_hbm.shape[1]
    FB = wg_hbm.shape[2] // B
    mb = lax.axis_index("bulk")
    me = lax.axis_index("expert")

    def bulk_at(k):
        return lax.rem(mb + k + B, B)

    def expert_at(k):
        return lax.rem(me + k + E, E)

    def weight_copy(i, k):
        if i == 2:
            rows = pl.ds(pl.multiple_of(bulk_at(-k) * FB, FB), FB)
            return pltpu.make_async_copy(wd_hbm.at[0, rows, :], wd.at[k], wsem.at[2, k])
        cols = pl.ds(pl.multiple_of(bulk_at(k) * FB, FB), FB)
        source, to = ((wg_hbm, wg), (wu_hbm, wu))[i]
        return pltpu.make_async_copy(source.at[0, :, cols], to.at[k], wsem.at[i, k])

    order = list(range(1, B)) + [0]
    barrier = pltpu.get_barrier_semaphore()
    for k in range(1, B):
        pl.semaphore_signal(barrier, inc=1, device_id=(bulk_at(k), me), device_id_type=MESH)
    for k in range(1, E):
        pl.semaphore_signal(barrier, inc=1, device_id=(mb, expert_at(k)), device_id_type=MESH)
    for k in order:
        weight_copy(0, k).start()
        weight_copy(1, k).start()
    for k in range(B):
        weight_copy(2, k).start()

    slot = lax.broadcasted_iota(jnp.int32, (T, SL), 1)
    slot_expert = lax.div(slot, CAP)
    slot_rank = slot - slot_expert * CAP
    named = jnp.zeros((T, SL), F32)
    gates = jnp.zeros((T, SL), F32)
    member = jnp.zeros((T, E), F32)
    e_iota = lax.broadcasted_iota(jnp.int32, (T, E), 1)
    for j in range(TOP):
        hit = ids[:, j : j + 1] == slot_expert
        named = named + jnp.where(hit, 1.0, 0.0)
        gates = gates + jnp.where(hit, gv[:, j : j + 1], 0.0)
        member = member + jnp.where(ids[:, j : j + 1] == e_iota, 1.0, 0.0)
    t_row = lax.broadcasted_iota(jnp.int32, (T, T), 0)
    t_col = lax.broadcasted_iota(jnp.int32, (T, T), 1)
    below = jnp.where(t_col < t_row, 1.0, 0.0).astype(BF)
    rank = dot(below, named.astype(BF))
    chosen = jnp.where(rank == slot_rank.astype(F32), named, 0.0)
    eye = jnp.where(
        lax.broadcasted_iota(jnp.int32, (SL, SL), 0) == lax.broadcasted_iota(jnp.int32, (SL, SL), 1),
        1.0,
        0.0,
    ).astype(BF)
    selector = lax.dot_general(
        eye, chosen.astype(BF), (((1,), (1,)), ((), ())), preferred_element_type=F32
    ).astype(BF)

    pl.semaphore_wait(barrier, B + E - 2)

    def send1(k):
        return pltpu.make_async_remote_copy(
            og.at[k], oin.at[k], s1.at[k], r1.at[k], device_id=(bulk_at(k), me), device_id_type=MESH
        )

    for k in order:
        cols = pl.ds(pl.multiple_of(bulk_at(k) * DS, 128), DS)
        rows = dot(selector, tok[:, cols]).astype(BF)
        if k:
            og[k] = rows
            send1(k).start()
        else:
            oin[0] = rows

    odd = lax.rem(lax.broadcasted_iota(jnp.int32, (T, E), 0), 2) == 1
    odd_count = jnp.sum(jnp.where(odd, member, 0.0), axis=0, keepdims=True)
    even_count = jnp.sum(jnp.where(odd, 0.0, member), axis=0, keepdims=True)
    er = lax.broadcasted_iota(jnp.int32, (E, E), 0)
    ec = lax.broadcasted_iota(jnp.int32, (E, E), 1)
    shift = jnp.where(lax.rem(er + 1, E) == ec, 1.0, 0.0).astype(BF)
    home = jnp.where(place[...] == ec, 1.0, 0.0).astype(BF)
    spread = lambda count, to: dot(jnp.broadcast_to(count, (8, E)).astype(BF), to)
    load[...] = (spread(odd_count, shift) + spread(even_count, home))[:1].astype(jnp.int32)
    combine = chosen * gates
    c_hi = combine.astype(BF)
    c_rest = combine - c_hi.astype(F32)
    c_mid = c_rest.astype(BF)
    c_lo = (c_rest - c_mid.astype(F32)).astype(BF)

    placed = dot(p1[mb], oin[0])
    for k in range(1, B):
        send1(k).wait_recv()
        placed = placed + dot(p1[bulk_at(-k)], oin[k])
    xs[...] = placed.astype(BF)

    def block(k):
        return pl.ds(pl.multiple_of(k * RP, RP), RP)

    def send2(k):
        return pltpu.make_async_remote_copy(
            xs.at[block(expert_at(k))], xr.at[block(k)], s2.at[k], r2.at[k],
            device_id=(mb, expert_at(k)), device_id_type=MESH,
        )

    for k in range(1, E):
        send2(k).start()
    xr[0:RP] = xs[block(me)]
    for k in range(1, E):
        send2(k).wait_recv()
    x[...] = dot(p2[...], xr[...]).astype(BF)

    def send3(k):
        return pltpu.make_async_remote_copy(
            pout.at[k], pin.at[k], s3.at[k], r3.at[k], device_id=(bulk_at(k), me), device_id_type=MESH
        )

    def partials(k, to):
        weight_copy(0, k).wait()
        weight_copy(1, k).wait()
        to[k, :, :FB] = dot(x[...], wg[k]).astype(BF)
        to[k, :, FB:] = dot(x[...], wu[k]).astype(BF)

    @pl.loop(1, B)
    def _(k):
        partials(k, pout)
        send3(k).start()

    partials(0, pin)
    total = pin[0].astype(F32)
    for k in range(1, B):
        send3(k).wait_recv()
        total = total + pin[k].astype(F32)
    gate = total[:, :FB]
    hin[0] = (gate / (1.0 + jnp.exp(-gate)) * total[:, FB:]).astype(BF)

    def send4(k):
        return pltpu.make_async_remote_copy(
            hin.at[0], hin.at[k], s4.at[k], r4.at[k], device_id=(bulk_at(k), me), device_id_type=MESH
        )

    for k in range(1, B):
        send4(k).start()
    weight_copy(2, 0).wait()
    acc[...] = dot(hin[0], wd[0])

    @pl.loop(1, B)
    def _(k):
        weight_copy(2, k).wait()
        send4(k).wait_recv()
        acc[...] += dot(hin[k], wd[k])

    for k in range(1, E):
        send2(k).wait_send()
    rr = xs
    rr[...] = dot(p2t[...], acc[...].astype(BF)).astype(BF)

    def send5(k):
        return pltpu.make_async_remote_copy(
            rr.at[block(k)], back.at[block(me)], s5.at[k], r5.at[k],
            device_id=(mb, expert_at(-k)), device_id_type=MESH,
        )

    for k in range(1, E):
        send5(k).start()
    back[block(me)] = rr[0:RP]
    for k in range(1, E):
        pltpu.make_async_remote_copy(
            rr.at[block(k)], back.at[block(expert_at(k))], s5.at[k], r5.at[k],
            device_id=(mb, expert_at(-k)), device_id_type=MESH,
        ).wait_recv()

    def send6(k):
        return pltpu.make_async_remote_copy(
            rb.at[k], fin.at[k], s6.at[k], r6.at[k], device_id=(bulk_at(k), me), device_id_type=MESH
        )

    for k in order:
        rows = dot(p1t[bulk_at(k)], back[...]).astype(BF)
        if k:
            rb[k] = rows
            send6(k).start()
        else:
            fin[0] = rows
    for k in range(B):
        if k:
            send6(k).wait_recv()
        rows = fin[k]
        cols = pl.ds(pl.multiple_of(bulk_at(-k) * DS, 128), DS)
        out[:, cols] = (dot(c_hi, rows) + (dot(c_mid, rows) + dot(c_lo, rows))).astype(BF)

    for k in range(1, B):
        send1(k).wait_send()
        send3(k).wait_send()
        send4(k).wait_send()
        send6(k).wait_send()
    for k in range(1, E):
        send5(k).wait_send()


def on_device(tokens, expert_ids, gate_values, placement, gate_weight, up_weight, down_weight):
    E = lax.axis_size("expert")
    B = lax.axis_size("bulk")
    T, D = tokens.shape
    DS = gate_weight.shape[1]
    FB = gate_weight.shape[2] // B
    SL = E * CAP
    RQ = B * CAP
    RP = -(-RQ // 16) * 16
    R = E * RQ
    p1 = np.zeros((B, E * RP, SL), np.float32)
    p2 = np.zeros((R, E * RP), np.float32)
    for e in range(E):
        for q in range(RQ):
            p1[q // CAP, e * RP + q, e * CAP + q % CAP] = 1.0
            p2[e * RQ + q, e * RP + q] = 1.0
    p1t = np.swapaxes(p1, 1, 2)
    consts = [jnp.asarray(a.astype(ml_dtypes.bfloat16)) for a in (p1, p1t, p2, p2.T)]
    vmem = pl.BlockSpec(memory_space=pltpu.VMEM)
    hbm = pl.BlockSpec(memory_space=pl.ANY)
    dma = pltpu.SemaphoreType.DMA
    return pl.pallas_call(
        functools.partial(kernel, B, E, RP),
        out_shape=(
            jax.ShapeDtypeStruct((T, D), BF),
            jax.ShapeDtypeStruct((1, E), jnp.int32),
        ),
        in_specs=[vmem] * 8 + [hbm] * 3,
        out_specs=(vmem, vmem),
        scratch_shapes=[
            pltpu.VMEM((B, DS, FB), BF),
            pltpu.VMEM((B, DS, FB), BF),
            pltpu.VMEM((B, FB, DS), BF),
            pltpu.VMEM((B, SL, DS), BF),
            pltpu.VMEM((B, SL, DS), BF),
            pltpu.VMEM((E * RP, DS), BF),
            pltpu.VMEM((E * RP, DS), BF),
            pltpu.VMEM((R, DS), BF),
            pltpu.VMEM((B, R, 2 * FB), BF),
            pltpu.VMEM((B, R, 2 * FB), BF),
            pltpu.VMEM((B, R, FB), BF),
            pltpu.VMEM((R, DS), F32),
            pltpu.VMEM((E * RP, DS), BF),
            pltpu.VMEM((B, SL, DS), BF),
            pltpu.VMEM((B, SL, DS), BF),
            dma((3, B)),
        ]
        + [dma((n,)) for n in (B, B, E, E, B, B, B, B, E, E, B, B)],
        compiler_params=pltpu.CompilerParams(
            collective_id=0, has_side_effects=True, vmem_limit_bytes=62 * 1024 * 1024
        ),
    )(tokens, expert_ids, gate_values, placement.reshape(E, 1), *consts,
      gate_weight, up_weight, down_weight)


def solution(mesh):
    placed = (
        P(("bulk", "expert"), None),
        P(("bulk", "expert"), None),
        P(("bulk", "expert"), None),
        P(),
        P("expert", "bulk", None),
        P("expert", "bulk", None),
        P("expert", None, "bulk"),
    )
    return jax.shard_map(
        on_device,
        mesh=mesh,
        in_specs=placed,
        out_specs=(P(("bulk", "expert"), None), P(("bulk", "expert"), None)),
        check_vma=False,
    )
```

time: 177 us -> 78.8 us (0.45)
  Pallas kernels: 0 us -> 70.4 us
  blocking collectives: 43 us -> 0 us
  local copies, waits for them, and re-layouts: 44.3 us -> 7.42 us
  waiting for transfers between devices: 36.3 us -> 0 us
  other arithmetic: 17.4 us -> 0 us
  between operations: 14.2 us -> 0.64 us
  matrix products: 13.5 us -> 0 us
  starting transfers between devices: 7.24 us -> 0 us
    pallas_call x0 -> x1, Pallas kernels: none -> 70.4 us  [on_device(): pl.pallas_call(functools.partial(kernel, B, E, RP), out_shape=(jax.ShapeD...]
    all_to_all x2 -> x0, blocking collectives: 28.1 us -> none  [the longest x1 16.7 us: on_device(): lax.all_to_all(outgoing, 'bulk', split_axis=3, concat_axis=0, tiled=True)]
    reduce_scatter x1 -> x0, waiting for transfers between devices: 20.5 us -> none  [expert_rows(): lax.psum_scatter(jnp.concatenate(pieces, axis=1).reshape(per_group * lax....]
    all_to_all x2 -> x0, waiting for transfers between devices: 15.8 us -> none  [the longest x1 9.02 us: on_device(): lax.all_to_all(lax.all_to_all(main_part, 'bulk', split_axis=0, concat_axi...]
    all_gather x1 -> x0, blocking collectives: 15 us -> none  [expert_rows(): lax.all_gather(hidden, 'bulk', axis=0, tiled=True)]
    reduce_sum x4 -> x0, other arithmetic: 13.6 us -> none  [the longest x1 12.8 us: on_device(): jnp.sum(weighted.reshape(tok_rows, top_count, model_width), axis=1)]
    dot_general x4 -> x0, matrix products: 13.5 us -> none  [the longest x1 4.41 us: expert_rows(): jnp.einsum('grd,df->grf', block_input, partial_weights_now[1], preferred_...]
    all_to_all x3 -> x0, local copies, waits for them, and re-layouts: 11 us -> none  [the longest x1 9.94 us: on_device(): lax.all_to_all(outgoing, 'bulk', split_axis=3, concat_axis=0, tiled=True)]
  transfers between devices with their start and end apart: 3 -> 0, of which waited for: 3 -> 0; matrix products, arithmetic and copies ran while one was open for 0% -> 0% of each run, Pallas kernels for 0% -> 0%
where the time goes in v1:
time: 78.8 us; the launch traced here: 78.5 us
  Pallas kernels  70.4 us (89%)
  local copies, waits for them, and re-layouts  7.42 us (9%)
    pallas_call x1, Pallas kernels, on_device(): pl.pallas_call(functools.partial(kernel, B, E, RP), out_shape=(jax.ShapeD...  70.4 us
    unnamed x4, local copies, waits for them, and re-layouts  6.1 us

profile of v1, /device:TPU:0, one launch (start us, length us, event | category | flops | bytes accessed | tf_op | source)
XLA Modules:
  0.0 78.5 jit_solution(2711810790023322145)
XLA Ops:
  0.6 1.3 %copy.15.place = s32[8,1]{1,0:T(8,128)} copy(s32[8,1]{0,1:T(1,128)} %bitcast.1) | data formatting | bytes 64 | tf_op jit(solution)/shard_map/reshape | solution.py:278
  1.9 1.4 %copy.13.ids = s32[64,8]{1,0:T(8,128)} copy(s32[64,8]{0,1:T(8,128)} %param.12) | data formatting | bytes 4096 | tf_op args[1]
  3.3 1.4 %copy.14.gv = f32[64,8]{1,0:T(8,128)} copy(f32[64,8]{0,1:T(8,128)} %param.13) | data formatting | bytes 4096 | tf_op args[2]
  4.7 70.4 %shard_map.122 = (bf16[64,7168]{1,0:T(8,128)(2,1)}, s32[1,8]{1,0:T(1,128)}) custom-call(bf16[64,7168]{1,0:T(8,128)(2,1)} %tok.1, s32[64,8]{1,0:T(8,128)} %copy.13.ids, f32[64,8]{1,0:T(8,128)} %copy.14.gv, s32[8,1]{1,0:T(8,128)} %copy.15.place, bf16[4,128,24]{2,1,0:T(8,128)(2,1)} %constant.8.clone.p1, bf16[4,24,128]{2,1,0:T(8,128)(2,1)} %constant.9.clone.p1t, ...), custom_call_target="tpu_custom_call" | custom-call | tf_op jit(solution)/shard_map/pallas_call | solution.py:248
  75.2 2.2 %copy.18 = bf16[64,7168]{1,0:T(8,128)(2,1)} copy(bf16[64,7168]{1,0:T(8,128)(2,1)} %get-tuple-element.4) | data formatting | bytes 1835008
  77.3 1.2 %copy.19 = s32[1,8]{1,0:T(1,128)} copy(s32[1,8]{1,0:T(1,128)} %get-tuple-element.5) | data formatting | bytes 64

commit v2 on v1

v2 whole, which is shorter than its diff:
```python
import functools

import jax
import jax.numpy as jnp
import ml_dtypes
import numpy as np
from jax import lax
from jax.experimental import pallas as pl
from jax.experimental.pallas import tpu as pltpu
from jax.sharding import PartitionSpec as P

CAP = 3
BF = jnp.bfloat16
F32 = jnp.float32
MESH = pl.DeviceIdType.MESH


def dot(a, b):
    return jnp.dot(a, b, preferred_element_type=F32)


def kernel(
    B, E, RP, H, G, tok_hbm, ids, gv, place, p1, p1t, p2, p2t, wg_hbm, wu_hbm, wd_hbm, out, load,
    tok, wg, wu, wd, og, oin, xs, xr, x, pout, pin, hin, acc, back, rb, fin,
    tsem, wsem, s1, r1, s2, r2, s3, r3, s4, r4, s5, r5, s6, r6,
):
    TOP, T = ids.shape
    SL = E * CAP
    DS = wg_hbm.shape[1]
    FB = wg_hbm.shape[2] // B
    DH = DS // H
    FH = FB // G
    mb = lax.axis_index("bulk")
    me = lax.axis_index("expert")

    def bulk_at(k):
        return lax.rem(mb + k + B, B)

    def expert_at(k):
        return lax.rem(me + k + E, E)

    def weight_copy(i, k):
        if i == 2:
            rows = pl.ds(pl.multiple_of(bulk_at(-k) * FB, FB), FB)
            return pltpu.make_async_copy(wd_hbm.at[0, rows, :], wd.at[k], wsem.at[2, k])
        cols = pl.ds(pl.multiple_of(bulk_at(k) * FB, FB), FB)
        source, to = ((wg_hbm, wg), (wu_hbm, wu))[i]
        return pltpu.make_async_copy(source.at[0, :, cols], to.at[k], wsem.at[i, k])

    tok_copy = pltpu.make_async_copy(tok_hbm, tok, tsem)
    tok_copy.start()
    far_first = [(i + B // 2 - 1) % (B - 1) + 1 for i in range(B - 1)]
    order = far_first + [0]
    barrier = pltpu.get_barrier_semaphore()
    for k in range(1, B):
        pl.semaphore_signal(barrier, inc=1, device_id=(bulk_at(k), me), device_id_type=MESH)
    for k in range(1, E):
        pl.semaphore_signal(barrier, inc=1, device_id=(mb, expert_at(k)), device_id_type=MESH)

    slot = lax.broadcasted_iota(jnp.int32, (SL, T), 0)
    slot_expert = lax.div(slot, CAP)
    slot_rank = slot - slot_expert * CAP
    named = jnp.zeros((SL, T), F32)
    gates = jnp.zeros((SL, T), F32)
    for j in range(TOP):
        hit = ids[j : j + 1, :] == slot_expert
        named = named + jnp.where(hit, 1.0, 0.0)
        gates = gates + jnp.where(hit, gv[j : j + 1, :], 0.0)
    t_row = lax.broadcasted_iota(jnp.int32, (T, T), 0)
    t_col = lax.broadcasted_iota(jnp.int32, (T, T), 1)
    before = jnp.where(t_row < t_col, 1.0, 0.0).astype(BF)
    rank = dot(named.astype(BF), before)
    chosen = jnp.where(rank == slot_rank.astype(F32), named, 0.0)
    selector = chosen.astype(BF)

    def send1(k, h):
        return pltpu.make_async_remote_copy(
            og.at[k, h], oin.at[k, h], s1.at[k, h], r1.at[k, h],
            device_id=(bulk_at(k), me), device_id_type=MESH,
        )

    pl.semaphore_wait(barrier, B + E - 2)
    tok_copy.wait()
    for h in range(H):
        for k in order:
            cols = pl.ds(pl.multiple_of(bulk_at(k) * DS + h * DH, 128), DH)
            rows = dot(selector, tok[:, cols]).astype(BF)
            if k:
                og[k, h] = rows
                send1(k, h).start()
            else:
                oin[0, h] = rows
    for k in order:
        weight_copy(0, k).start()
        weight_copy(1, k).start()
    for k in range(B):
        weight_copy(2, k).start()

    member = jnp.zeros((E, T), F32)
    e_iota = lax.broadcasted_iota(jnp.int32, (E, T), 0)
    for j in range(TOP):
        member = member + jnp.where(ids[j : j + 1, :] == e_iota, 1.0, 0.0)
    odd_t = lax.rem(lax.broadcasted_iota(jnp.int32, (8, T), 1), 2) == 1
    odd = jnp.where(odd_t, 1.0, 0.0).astype(BF)
    even = jnp.where(odd_t, 0.0, 1.0).astype(BF)
    er = lax.broadcasted_iota(jnp.int32, (E, E), 0)
    ec = lax.broadcasted_iota(jnp.int32, (E, E), 1)
    shift = jnp.where(er == lax.rem(ec + 1, E), 1.0, 0.0).astype(BF)
    home = jnp.where(er == place[...], 1.0, 0.0).astype(BF)

    def across(a, b):
        return lax.dot_general(a, b, (((1,), (1,)), ((), ())), preferred_element_type=F32)

    member = member.astype(BF)
    loads = across(across(odd, member).astype(BF), shift) + across(
        across(even, member).astype(BF), home
    )
    load[...] = loads[:1].astype(jnp.int32)
    eye = jnp.where(t_row == t_col, 1.0, 0.0).astype(BF)
    combine = chosen * gates
    c_hi = combine.astype(BF)
    c_rest = combine - c_hi.astype(F32)
    c_mid = c_rest.astype(BF)
    c_lo = (c_rest - c_mid.astype(F32)).astype(BF)
    c_hi, c_mid, c_lo = (across(eye, c).astype(BF) for c in (c_hi, c_mid, c_lo))

    def block(k):
        return pl.ds(pl.multiple_of(k * RP, RP), RP)

    def send2(k, h):
        return pltpu.make_async_remote_copy(
            xs.at[h, block(expert_at(k))], xr.at[h, block(k)], s2.at[k, h], r2.at[k, h],
            device_id=(mb, expert_at(k)), device_id_type=MESH,
        )

    for h in range(H):
        rows = dot(p1[mb], oin[0, h])
        for k in range(1, B):
            send1(k, h).wait_recv()
            rows = rows + dot(p1[bulk_at(-k)], oin[k, h])
        xs[h] = rows.astype(BF)
        for k in range(1, E):
            send2(k, h).start()
        xr[h, 0:RP] = xs[h, block(me)]
    for h in range(H):
        for k in range(1, E):
            send2(k, h).wait_recv()
        x[:, h * DH : (h + 1) * DH] = dot(p2[...], xr[h]).astype(BF)

    def send3(k, q):
        return pltpu.make_async_remote_copy(
            pout.at[q, k], pin.at[q, k], s3.at[k, q], r3.at[k, q],
            device_id=(bulk_at(k), me), device_id_type=MESH,
        )

    def partials(k, q, to):
        cols = slice(q * FH, (q + 1) * FH)
        to[q, k, :, :FH] = dot(x[...], wg[k, :, cols]).astype(BF)
        to[q, k, :, FH:] = dot(x[...], wu[k, :, cols]).astype(BF)

    for q in range(G):

        @pl.loop(0, B - 1)
        def _(i):
            k = lax.rem(i + (B // 2 - 1), B - 1) + 1
            if q == 0:
                weight_copy(0, k).wait()
                weight_copy(1, k).wait()
            partials(k, q, pout)
            send3(k, q).start()

    weight_copy(0, 0).wait()
    weight_copy(1, 0).wait()

    def send4(k, q):
        return pltpu.make_async_remote_copy(
            hin.at[q, 0], hin.at[q, k], s4.at[k, q], r4.at[k, q],
            device_id=(bulk_at(k), me), device_id_type=MESH,
        )

    for q in range(G):
        partials(0, q, pin)
    for q in range(G):
        total = pin[q, 0].astype(F32)
        for k in range(1, B):
            send3(k, q).wait_recv()
            total = total + pin[q, k].astype(F32)
        gate = total[:, :FH]
        hin[q, 0] = (gate / (1.0 + jnp.exp(-gate)) * total[:, FH:]).astype(BF)
        for k in far_first:
            send4(k, q).start()
    weight_copy(2, 0).wait()
    acc[...] = dot(hin[0, 0], wd[0, 0:FH])
    for q in range(1, G):
        acc[...] += dot(hin[q, 0], wd[0, q * FH : (q + 1) * FH])
    for k in range(1, B):
        weight_copy(2, k).wait()
    for q in range(G):

        @pl.loop(1, B - 1 if q == G - 1 else B)
        def _(k):
            send4(k, q).wait_recv()
            acc[...] += dot(hin[q, k], wd[k, q * FH : (q + 1) * FH])

    rr = xs

    def send5(k, h, at):
        return pltpu.make_async_remote_copy(
            rr.at[h, block(k)], back.at[h, block(at)], s5.at[k, h], r5.at[k, h],
            device_id=(mb, expert_at(-k)), device_id_type=MESH,
        )

    send4(B - 1, G - 1).wait_recv()
    for h in range(H):
        for k in range(1, E):
            send2(k, h).wait_send()
        cols = slice(h * DH, (h + 1) * DH)
        rows = acc[:, cols] + dot(hin[G - 1, B - 1], wd[B - 1, (G - 1) * FH : G * FH, cols])
        rr[h] = dot(p2t[...], rows.astype(BF)).astype(BF)
        for k in range(1, E):
            send5(k, h, me).start()
        back[h, block(me)] = rr[h, 0:RP]

    def send6(k, h):
        return pltpu.make_async_remote_copy(
            rb.at[k, h], fin.at[k, h], s6.at[k, h], r6.at[k, h],
            device_id=(bulk_at(k), me), device_id_type=MESH,
        )

    for h in range(H):
        for k in range(1, E):
            send5(k, h, expert_at(k)).wait_recv()
        for k in order:
            rows = dot(p1t[bulk_at(k)], back[h]).astype(BF)
            if k:
                rb[k, h] = rows
                send6(k, h).start()
            else:
                fin[0, h] = rows
    for h in range(H):
        for k in range(B):
            if k:
                send6(k, h).wait_recv()
            rows = fin[k, h]
            cols = pl.ds(pl.multiple_of(bulk_at(-k) * DS + h * DH, 128), DH)
            out[:, cols] = (dot(c_hi, rows) + (dot(c_mid, rows) + dot(c_lo, rows))).astype(BF)

    for k in range(1, B):
        for h in range(H):
            send1(k, h).wait_send()
            send6(k, h).wait_send()
        for q in range(G):
            send3(k, q).wait_send()
            send4(k, q).wait_send()
    for k in range(1, E):
        for h in range(H):
            send5(k, h, me).wait_send()


def on_device(tokens, expert_ids, gate_values, placement, gate_weight, up_weight, down_weight):
    E = lax.axis_size("expert")
    B = lax.axis_size("bulk")
    T, D = tokens.shape
    DS = gate_weight.shape[1]
    FB = gate_weight.shape[2] // B
    SL = E * CAP
    RQ = B * CAP
    RP = -(-RQ // 16) * 16
    R = E * RQ
    p1 = np.zeros((B, E * RP, SL), np.float32)
    p2 = np.zeros((R, E * RP), np.float32)
    for e in range(E):
        for q in range(RQ):
            p1[q // CAP, e * RP + q, e * CAP + q % CAP] = 1.0
            p2[e * RQ + q, e * RP + q] = 1.0
    p1t = np.swapaxes(p1, 1, 2)
    consts = [jnp.asarray(a.astype(ml_dtypes.bfloat16)) for a in (p1, p1t, p2, p2.T)]
    H = 2 if DS % 256 == 0 else 1
    G = 2 if FB % 256 == 0 else 1
    DH = DS // H
    FH = FB // G
    vmem = pl.BlockSpec(memory_space=pltpu.VMEM)
    hbm = pl.BlockSpec(memory_space=pl.ANY)
    dma = pltpu.SemaphoreType.DMA
    buffers = [
        (T, D), (B, DS, FB), (B, DS, FB), (B, FB, DS),
        (B, H, SL, DH), (B, H, SL, DH), (H, E * RP, DH), (H, E * RP, DH), (R, DS),
        (G, B, R, 2 * FH), (G, B, R, 2 * FH), (G, B, R, FH), (R, DS),
        (H, E * RP, DH), (B, H, SL, DH), (B, H, SL, DH),
    ]
    sems = [(B, H), (B, H), (E, H), (E, H)] + [(B, G)] * 4 + [(E, H), (E, H), (B, H), (B, H)]
    return pl.pallas_call(
        functools.partial(kernel, B, E, RP, H, G),
        out_shape=(
            jax.ShapeDtypeStruct((T, D), BF),
            jax.ShapeDtypeStruct((1, E), jnp.int32),
        ),
        in_specs=[hbm] + [vmem] * 7 + [hbm] * 3,
        out_specs=(vmem, vmem),
        scratch_shapes=[pltpu.VMEM(d, F32 if i == 12 else BF) for i, d in enumerate(buffers)]
        + [dma, dma((3, B))]
        + [dma(n) for n in sems],
        compiler_params=pltpu.CompilerParams(
            collective_id=0, has_side_effects=True, vmem_limit_bytes=62 * 1024 * 1024
        ),
    )(tokens, expert_ids.T, gate_values.T, placement.reshape(1, E), *consts,
      gate_weight, up_weight, down_weight)


def solution(mesh):
    placed = (
        P(("bulk", "expert"), None),
        P(("bulk", "expert"), None),
        P(("bulk", "expert"), None),
        P(),
        P("expert", "bulk", None),
        P("expert", "bulk", None),
        P("expert", None, "bulk"),
    )
    return jax.shard_map(
        on_device,
        mesh=mesh,
        in_specs=placed,
        out_specs=(P(("bulk", "expert"), None), P(("bulk", "expert"), None)),
        check_vma=False,
    )
```

time: 78.8 us -> 69.6 us (0.88)
  Pallas kernels: 70.4 us -> 65.4 us
  local copies, waits for them, and re-layouts: 7.42 us -> 3.33 us
    pallas_call x1, Pallas kernels: 70.4 us -> 65.4 us  [on_device(): pl.pallas_call(functools.partial(kernel, B, E, RP, H, G), out_shape=(jax....]
    unnamed x4 -> x2, local copies, waits for them, and re-layouts: 6.1 us -> 3.33 us
    reshape x1 -> x0, local copies, waits for them, and re-layouts: 1.32 us -> none  [on_device(): placement.reshape(E, 1)]
where the time goes in v2:
time: 69.6 us; the launch traced here: 69.4 us
  Pallas kernels  65.4 us (94%)
  local copies, waits for them, and re-layouts  3.33 us (5%)
    pallas_call x1, Pallas kernels, on_device(): pl.pallas_call(functools.partial(kernel, B, E, RP, H, G), out_shape=(jax....  65.4 us
    unnamed x2, local copies, waits for them, and re-layouts  3.33 us

profile of v2, /device:TPU:0, one launch (start us, length us, event | category | flops | bytes accessed | tf_op | source)
XLA Modules:
  0.0 69.4 jit_solution(12224571496786466423)
XLA Ops:
  0.6 65.4 %shard_map.122 = (bf16[64,7168]{1,0:T(8,128)(2,1)}, s32[1,8]{1,0:T(1,128)}) custom-call(bf16[64,7168]{1,0:T(8,128)(2,1)} %tok_hbm.1, s32[8,64]{1,0:T(8,128)} %bitcast.3, f32[8,64]{1,0:T(8,128)} %bitcast.4, s32[1,8]{1,0:T(1,128)} %bitcast.5, bf16[4,128,24]{2,1,0:T(8,128)(2,1)} %constant.8.clone.p1, bf16[4,24,128]{2,1,0:T(8,128)(2,1)} %constant.9.clone.p1t, ...), custom_call_target="tpu_custom_call" | custom-call | tf_op jit(solution)/shard_map/pallas_call | solution.py:292
  66.0 2.2 %copy.15 = bf16[64,7168]{1,0:T(8,128)(2,1)} copy(bf16[64,7168]{1,0:T(8,128)(2,1)} %get-tuple-element.4) | data formatting | bytes 1835008
  68.2 1.2 %copy.16 = s32[1,8]{1,0:T(1,128)} copy(s32[1,8]{1,0:T(1,128)} %get-tuple-element.5) | data formatting | bytes 64

commit v3 on v2

--- a/solution.py
+++ b/solution.py
@@ -20,9 +20,9 @@
 
 
 def kernel(
-    B, E, RP, H, G, tok_hbm, ids, gv, place, p1, p1t, p2, p2t, wg_hbm, wu_hbm, wd_hbm, out, load,
-    tok, wg, wu, wd, og, oin, xs, xr, x, pout, pin, hin, acc, back, rb, fin,
-    tsem, wsem, s1, r1, s2, r2, s3, r3, s4, r4, s5, r5, s6, r6,
+    B, E, RP, H, G, tok_hbm, ids, gv, place, p1, p1t, p2, p2t, wg_hbm, wu_hbm, wd_hbm,
+    fin, cs, ld, tok, wg, wu, wd, og, oin, xs, xr, x, pout, pin, hin, acc, back, rb, csv, ldv,
+    tsem, csem, fsem, wsem, s1, r1, s2, r2, s3, r3, s4, r4, s5, r5, s6, r6,
 ):
     TOP, T = ids.shape
     SL = E * CAP
@@ -115,14 +115,21 @@
     loads = across(across(odd, member).astype(BF), shift) + across(
         across(even, member).astype(BF), home
     )
-    load[...] = loads[:1].astype(jnp.int32)
+    ldv[...] = loads
     eye = jnp.where(t_row == t_col, 1.0, 0.0).astype(BF)
     combine = chosen * gates
     c_hi = combine.astype(BF)
     c_rest = combine - c_hi.astype(F32)
     c_mid = c_rest.astype(BF)
     c_lo = (c_rest - c_mid.astype(F32)).astype(BF)
-    c_hi, c_mid, c_lo = (across(eye, c).astype(BF) for c in (c_hi, c_mid, c_lo))
+    for i, c in enumerate((c_hi, c_mid, c_lo)):
+        csv[i] = across(eye, c).astype(BF)
+    side = (
+        pltpu.make_async_copy(csv, cs, csem.at[0]),
+        pltpu.make_async_copy(ldv, ld, csem.at[1]),
+    )
+    for copy in side:
+        copy.start()
 
     def block(k):
         return pl.ds(pl.multiple_of(k * RP, RP), RP)
@@ -221,40 +228,58 @@
             send5(k, h, me).start()
         back[h, block(me)] = rr[h, 0:RP]
 
-    def send6(k, h):
-        return pltpu.make_async_remote_copy(
-            rb.at[k, h], fin.at[k, h], s6.at[k, h], r6.at[k, h],
+    def send6(k, h, at):
+        return pltpu.make_async_remote_copy(
+            rb.at[k, h], fin.at[at, h], s6.at[k, h], r6.at[k, h],
             device_id=(bulk_at(k), me), device_id_type=MESH,
         )
+
+    def keep(h):
+        return pltpu.make_async_copy(rb.at[0, h], fin.at[mb, h], fsem.at[h])
 
     for h in range(H):
         for k in range(1, E):
             send5(k, h, expert_at(k)).wait_recv()
         for k in order:
-            rows = dot(p1t[bulk_at(k)], back[h]).astype(BF)
+            rb[k, h] = dot(p1t[bulk_at(k)], back[h]).astype(BF)
             if k:
-                rb[k, h] = rows
-                send6(k, h).start()
+                send6(k, h, mb).start()
             else:
-                fin[0, h] = rows
-    for h in range(H):
-        for k in range(B):
-            if k:
-                send6(k, h).wait_recv()
-            rows = fin[k, h]
-            cols = pl.ds(pl.multiple_of(bulk_at(-k) * DS + h * DH, 128), DH)
-            out[:, cols] = (dot(c_hi, rows) + (dot(c_mid, rows) + dot(c_lo, rows))).astype(BF)
-
+                keep(h).start()
+    for copy in side:
+        copy.wait()
     for k in range(1, B):
         for h in range(H):
             send1(k, h).wait_send()
-            send6(k, h).wait_send()
+            send6(k, h, mb).wait_send()
         for q in range(G):
             send3(k, q).wait_send()
             send4(k, q).wait_send()
     for k in range(1, E):
         for h in range(H):
             send5(k, h, me).wait_send()
+    for h in range(H):
+        keep(h).wait()
+        for k in range(1, B):
+            send6(k, h, bulk_at(-k)).wait_recv()
+
+
+def combine_kernel(fin, cs, ld, out_hbm, load, out, sems):
+    B, H, SL, DH = fin.shape
+    load[...] = ld[:1].astype(jnp.int32)
+    copies = []
+    for b in range(B):
+        for h in range(H):
+            rows = fin[b, h]
+            at = (b * H + h) * DH
+            out[:, at : at + DH] = (
+                dot(cs[0], rows) + (dot(cs[1], rows) + dot(cs[2], rows))
+            ).astype(BF)
+        cols = pl.ds(b * H * DH, H * DH)
+        copies.append(pltpu.make_async_copy(out.at[:, cols], out_hbm.at[:, cols], sems.at[b]))
+        copies[-1].start()
+    for copy in copies:
+        copy.wait()
 
 
 def on_device(tokens, expert_ids, gate_values, placement, gate_weight, up_weight, down_weight):
@@ -286,25 +311,36 @@
         (T, D), (B, DS, FB), (B, DS, FB), (B, FB, DS),
         (B, H, SL, DH), (B, H, SL, DH), (H, E * RP, DH), (H, E * RP, DH), (R, DS),
         (G, B, R, 2 * FH), (G, B, R, 2 * FH), (G, B, R, FH), (R, DS),
-        (H, E * RP, DH), (B, H, SL, DH), (B, H, SL, DH),
+        (H, E * RP, DH), (B, H, SL, DH), (3, T, SL), (8, E),
     ]
     sems = [(B, H), (B, H), (E, H), (E, H)] + [(B, G)] * 4 + [(E, H), (E, H), (B, H), (B, H)]
-    return pl.pallas_call(
+    fin, cs, ld = pl.pallas_call(
         functools.partial(kernel, B, E, RP, H, G),
         out_shape=(
-            jax.ShapeDtypeStruct((T, D), BF),
-            jax.ShapeDtypeStruct((1, E), jnp.int32),
+            jax.ShapeDtypeStruct((B, H, SL, DH), BF),
+            jax.ShapeDtypeStruct((3, T, SL), BF),
+            jax.ShapeDtypeStruct((8, E), F32),
         ),
         in_specs=[hbm] + [vmem] * 7 + [hbm] * 3,
-        out_specs=(vmem, vmem),
-        scratch_shapes=[pltpu.VMEM(d, F32 if i == 12 else BF) for i, d in enumerate(buffers)]
-        + [dma, dma((3, B))]
+        out_specs=(hbm, hbm, hbm),
+        scratch_shapes=[pltpu.VMEM(d, F32 if i in (12, 16) else BF) for i, d in enumerate(buffers)]
+        + [dma, dma((2,)), dma((H,)), dma((3, B))]
         + [dma(n) for n in sems],
         compiler_params=pltpu.CompilerParams(
             collective_id=0, has_side_effects=True, vmem_limit_bytes=62 * 1024 * 1024
         ),
     )(tokens, expert_ids.T, gate_values.T, placement.reshape(1, E), *consts,
       gate_weight, up_weight, down_weight)
+    return pl.pallas_call(
+        combine_kernel,
+        out_shape=(
+            jax.ShapeDtypeStruct((T, D), BF),
+            jax.ShapeDtypeStruct((1, E), jnp.int32),
+        ),
+        in_specs=[vmem] * 3,
+        out_specs=(hbm, vmem),
+        scratch_shapes=[pltpu.VMEM((T, D), BF), dma((B,))],
+    )(fin, cs, ld)
 
 
 def solution(mesh):

time: 69.6 us -> 68 us (0.977)
  local copies, waits for them, and re-layouts: 3.33 us -> 0 us
  Pallas kernels: 65.4 us -> 67.2 us
    unnamed x2 -> x0, local copies, waits for them, and re-layouts: 3.33 us -> none
    pallas_call x0 -> x1, Pallas kernels: none -> 3.08 us  [on_device(): pl.pallas_call(combine_kernel, out_shape=(jax.ShapeDtypeStruct((T, D), BF...]
    pallas_call x1, Pallas kernels: 65.4 us -> 64.1 us  [on_device(): pl.pallas_call(functools.partial(kernel, B, E, RP, H, G), out_shape=(jax....]
where the time goes in v3:
time: 68 us; the launch traced here: 67.8 us
  Pallas kernels  67.2 us (99%)
    pallas_call x1, Pallas kernels, on_device(): pl.pallas_call(functools.partial(kernel, B, E, RP, H, G), out_shape=(jax....  64.1 us
    pallas_call x1, Pallas kernels, on_device(): pl.pallas_call(combine_kernel, out_shape=(jax.ShapeDtypeStruct((T, D), BF...  3.08 us

profile of v3, /device:TPU:0, one launch (start us, length us, event | category | flops | bytes accessed | tf_op | source)
XLA Modules:
  0.0 67.8 jit_solution(14404492523875429345)
XLA Ops:
  0.6 64.1 %shard_map.122 = (bf16[4,2,24,896]{3,2,1,0:T(8,128)(2,1)}, bf16[3,64,24]{2,1,0:T(8,128)(2,1)}, f32[8,8]{1,0:T(8,128)}) custom-call(bf16[64,7168]{1,0:T(8,128)(2,1)} %tok_hbm.1, s32[8,64]{1,0:T(8,128)} %bitcast.3, f32[8,64]{1,0:T(8,128)} %bitcast.4, s32[1,8]{1,0:T(1,128)} %bitcast.5, bf16[4,128,24]{2,1,0:T(8,128)(2,1)} %constant.8.clone.p1, ...), custom_call_target="tpu_custom_call" | custom-call | tf_op jit(solution)/shard_map/pallas_call | solution.py:317
  64.7 3.1 %shard_map.123 = (bf16[64,7168]{1,0:T(8,128)(2,1)}, s32[1,8]{1,0:T(1,128)}) custom-call(bf16[4,2,24,896]{3,2,1,0:T(8,128)(2,1)} %get-tuple-element.5.fin, bf16[3,64,24]{2,1,0:T(8,128)(2,1)} %get-tuple-element.6.cs, f32[8,8]{1,0:T(8,128)} %get-tuple-element.7.ld), custom_call_target="tpu_custom_call" | custom-call | tf_op jit(solution)/shard_map/pallas_call | solution.py:334

commit v4 on v3

--- a/solution.py
+++ b/solution.py
@@ -154,30 +154,72 @@
             send2(k, h).wait_recv()
         x[:, h * DH : (h + 1) * DH] = dot(p2[...], xr[h]).astype(BF)
 
-    def send3(k, q):
-        return pltpu.make_async_remote_copy(
-            pout.at[q, k], pin.at[q, k], s3.at[k, q], r3.at[k, q],
-            device_id=(bulk_at(k), me), device_id_type=MESH,
-        )
-
-    def partials(k, q, to):
+    pair = lax.div(mb, 2)
+    is_odd = lax.rem(mb, 2)
+    partner = mb + 1 - 2 * is_odd
+
+    def direct(d, q):
+        return pltpu.make_async_remote_copy(
+            pout.at[q, d], pin.at[q, pair], s3.at[d, q], r3.at[pair, q],
+            device_id=(d, me), device_id_type=MESH,
+        )
+
+    def relay(d, q):
+        return pltpu.make_async_remote_copy(
+            pout.at[q, d], pin.at[q, B // 2 + d], s3.at[d, q], r3.at[B // 2 + d, q],
+            device_id=(partner, me), device_id_type=MESH,
+        )
+
+    def arrival(p, q):
+        return pltpu.make_async_remote_copy(
+            pout.at[q, mb], pin.at[q, p], s3.at[mb, q], r3.at[p, q],
+            device_id=(partner, me), device_id_type=MESH,
+        )
+
+    def above(d):
+        return jnp.where(lax.div(d, 2) > pair, 1, 0)
+
+    def partials(d, k, q):
         cols = slice(q * FH, (q + 1) * FH)
-        to[q, k, :, :FH] = dot(x[...], wg[k, :, cols]).astype(BF)
-        to[q, k, :, FH:] = dot(x[...], wu[k, :, cols]).astype(BF)
+        pout[q, d, :, :FH] = dot(x[...], wg[k, :, cols]).astype(BF)
+        pout[q, d, :, FH:] = dot(x[...], wu[k, :, cols]).astype(BF)
 
     for q in range(G):
 
         @pl.loop(0, B - 1)
         def _(i):
             k = lax.rem(i + (B // 2 - 1), B - 1) + 1
+            d = bulk_at(k)
             if q == 0:
                 weight_copy(0, k).wait()
                 weight_copy(1, k).wait()
-            partials(k, q, pout)
-            send3(k, q).start()
+            partials(d, k, q)
+
+            @pl.when(d == partner)
+            def _():
+                direct(d, q).start()
+
+            @pl.when((d != partner) & (above(d) != is_odd))
+            def _():
+                relay(d, q).start()
 
     weight_copy(0, 0).wait()
     weight_copy(1, 0).wait()
+    for q in range(G):
+        partials(mb, 0, q)
+
+    for q in range(G):
+
+        @pl.loop(0, B - 1)
+        def _(i):
+            d = bulk_at(lax.rem(i + (B // 2 - 1), B - 1) + 1)
+
+            @pl.when((d != partner) & (above(d) == is_odd))
+            def _():
+                arrival(B // 2 + d, q).wait_recv()
+                both = pout[q, d].astype(F32) + pin[q, B // 2 + d].astype(F32)
+                pout[q, d] = both.astype(BF)
+                direct(d, q).start()
 
     def send4(k, q):
         return pltpu.make_async_remote_copy(
@@ -186,12 +228,10 @@
         )
 
     for q in range(G):
-        partials(0, q, pin)
-    for q in range(G):
-        total = pin[q, 0].astype(F32)
-        for k in range(1, B):
-            send3(k, q).wait_recv()
-            total = total + pin[q, k].astype(F32)
+        total = pout[q, mb].astype(F32)
+        for p in range(B // 2):
+            arrival(p, q).wait_recv()
+            total = total + pin[q, p].astype(F32)
         gate = total[:, :FH]
         hin[q, 0] = (gate / (1.0 + jnp.exp(-gate)) * total[:, FH:]).astype(BF)
         for k in far_first:
@@ -253,7 +293,7 @@
             send1(k, h).wait_send()
             send6(k, h, mb).wait_send()
         for q in range(G):
-            send3(k, q).wait_send()
+            direct(bulk_at(k), q).wait_send()
             send4(k, q).wait_send()
     for k in range(1, E):
         for h in range(H):
@@ -310,10 +350,10 @@
     buffers = [
         (T, D), (B, DS, FB), (B, DS, FB), (B, FB, DS),
         (B, H, SL, DH), (B, H, SL, DH), (H, E * RP, DH), (H, E * RP, DH), (R, DS),
-        (G, B, R, 2 * FH), (G, B, R, 2 * FH), (G, B, R, FH), (R, DS),
+        (G, B, R, 2 * FH), (G, B + B // 2, R, 2 * FH), (G, B, R, FH), (R, DS),
         (H, E * RP, DH), (B, H, SL, DH), (3, T, SL), (8, E),
     ]
-    sems = [(B, H), (B, H), (E, H), (E, H)] + [(B, G)] * 4 + [(E, H), (E, H), (B, H), (B, H)]
+    sems = [(B, H), (B, H), (E, H), (E, H)] + [(B, G), (B + B // 2, G), (B, G), (B, G)] + [(E, H), (E, H), (B, H), (B, H)]
     fin, cs, ld = pl.pallas_call(
         functools.partial(kernel, B, E, RP, H, G),
         out_shape=(

time: 68 us -> 67.1 us (0.987)
  Pallas kernels: 67.2 us -> 66.3 us
    pallas_call x1, Pallas kernels: 64.1 us -> 63.2 us  [on_device(): pl.pallas_call(functools.partial(kernel, B, E, RP, H, G), out_shape=(jax....]
where the time goes in v4:
time: 67.1 us; the launch traced here: 67 us
  Pallas kernels  66.3 us (99%)
    pallas_call x1, Pallas kernels, on_device(): pl.pallas_call(functools.partial(kernel, B, E, RP, H, G), out_shape=(jax....  63.2 us
    pallas_call x1, Pallas kernels, on_device(): pl.pallas_call(combine_kernel, out_shape=(jax.ShapeDtypeStruct((T, D), BF...  3.09 us

profile of v4, /device:TPU:0, one launch (start us, length us, event | category | flops | bytes accessed | tf_op | source)
XLA Modules:
  0.0 67.0 jit_solution(16427765464272420981)
XLA Ops:
  0.6 63.2 %shard_map.122 = (bf16[4,2,24,896]{3,2,1,0:T(8,128)(2,1)}, bf16[3,64,24]{2,1,0:T(8,128)(2,1)}, f32[8,8]{1,0:T(8,128)}) custom-call(bf16[64,7168]{1,0:T(8,128)(2,1)} %tok_hbm.1, s32[8,64]{1,0:T(8,128)} %bitcast.3, f32[8,64]{1,0:T(8,128)} %bitcast.4, s32[1,8]{1,0:T(1,128)} %bitcast.5, bf16[4,128,24]{2,1,0:T(8,128)(2,1)} %constant.8.clone.p1, ...), custom_call_target="tpu_custom_call" | custom-call | tf_op jit(solution)/shard_map/pallas_call | solution.py:357
  63.9 3.1 %shard_map.123 = (bf16[64,7168]{1,0:T(8,128)(2,1)}, s32[1,8]{1,0:T(1,128)}) custom-call(bf16[4,2,24,896]{3,2,1,0:T(8,128)(2,1)} %get-tuple-element.5.fin, bf16[3,64,24]{2,1,0:T(8,128)(2,1)} %get-tuple-element.6.cs, f32[8,8]{1,0:T(8,128)} %get-tuple-element.7.ld), custom_call_target="tpu_custom_call" | custom-call | tf_op jit(solution)/shard_map/pallas_call | solution.py:374

commit v5 on v4

--- a/solution.py
+++ b/solution.py
@@ -188,8 +188,8 @@
 
         @pl.loop(0, B - 1)
         def _(i):
-            k = lax.rem(i + (B // 2 - 1), B - 1) + 1
-            d = bulk_at(k)
+            d = jnp.where(i < B - 2, lax.rem(2 * pair + 2 + i, B), partner)
+            k = lax.rem(d - mb + B, B)
             if q == 0:
                 weight_copy(0, k).wait()
                 weight_copy(1, k).wait()
@@ -212,7 +212,7 @@
 
         @pl.loop(0, B - 1)
         def _(i):
-            d = bulk_at(lax.rem(i + (B // 2 - 1), B - 1) + 1)
+            d = jnp.where(i < B - 2, lax.rem(2 * pair + 2 + i, B), partner)
 
             @pl.when((d != partner) & (above(d) == is_odd))
             def _():

time: 67.1 us -> 65.5 us (0.976)
  Pallas kernels: 66.3 us -> 64.7 us
    pallas_call x1, Pallas kernels: 63.2 us -> 61.6 us  [on_device(): pl.pallas_call(functools.partial(kernel, B, E, RP, H, G), out_shape=(jax....]
where the time goes in v5:
time: 65.5 us; the launch traced here: 65.4 us
  Pallas kernels  64.7 us (99%)
    pallas_call x1, Pallas kernels, on_device(): pl.pallas_call(functools.partial(kernel, B, E, RP, H, G), out_shape=(jax....  61.6 us
    pallas_call x1, Pallas kernels, on_device(): pl.pallas_call(combine_kernel, out_shape=(jax.ShapeDtypeStruct((T, D), BF...  3.09 us

profile of v5, /device:TPU:0, one launch (start us, length us, event | category | flops | bytes accessed | tf_op | source)
XLA Modules:
  0.0 65.4 jit_solution(7494262533075784625)
XLA Ops:
  0.6 61.6 %shard_map.122 = (bf16[4,2,24,896]{3,2,1,0:T(8,128)(2,1)}, bf16[3,64,24]{2,1,0:T(8,128)(2,1)}, f32[8,8]{1,0:T(8,128)}) custom-call(bf16[64,7168]{1,0:T(8,128)(2,1)} %tok_hbm.1, s32[8,64]{1,0:T(8,128)} %bitcast.3, f32[8,64]{1,0:T(8,128)} %bitcast.4, s32[1,8]{1,0:T(1,128)} %bitcast.5, bf16[4,128,24]{2,1,0:T(8,128)(2,1)} %constant.8.clone.p1, ...), custom_call_target="tpu_custom_call" | custom-call | tf_op jit(solution)/shard_map/pallas_call | solution.py:357
  62.3 3.1 %shard_map.123 = (bf16[64,7168]{1,0:T(8,128)(2,1)}, s32[1,8]{1,0:T(1,128)}) custom-call(bf16[4,2,24,896]{3,2,1,0:T(8,128)(2,1)} %get-tuple-element.5.fin, bf16[3,64,24]{2,1,0:T(8,128)(2,1)} %get-tuple-element.6.cs, f32[8,8]{1,0:T(8,128)} %get-tuple-element.7.ld), custom_call_target="tpu_custom_call" | custom-call | tf_op jit(solution)/shard_map/pallas_call | solution.py:374
